TPU v7x, 256 devices: a whole 4x4x8 slice. The times are simulated.
256 devices in a mesh: row: 4 (over x), col: 16 (over y, z_lo), gz: 4 (over z_hi, core).
Axes of the slice: x: 4, y: 4, z: 8 (z_hi: 2, z_lo: 4; z = z_hi * 4 + z_lo), core: 2. Of those that a mesh axis runs over, the one named last changes fastest.
Arguments:
- volume_field: bfloat16 [128, 32, 128, 512], P(None, 'row', 'col', 'gz'), may hold values from -6 to 6
- volume_load: bfloat16 [128, 32, 128, 512], P(None, 'row', 'col', 'gz'), may hold values from -6 to 6
- coefficient: float32 [32, 128, 512], P('row', 'col', 'gz'), may hold values from 0.25 to 2
- surface_block: bfloat16 [1024, 262144], P('row', 'col'), may hold values from -0.015625 to 0.015625
- trace_cell: int32 [4, 16, 4, 1024], P('row', 'col', 'gz'), may hold values from 0 to 8191, as said below
- flux_cell: int32 [4, 16, 4, 4], P('row', 'col', 'gz'), may hold values from 0 to 8191, as said below
Outputs:
- new_field: bfloat16 [128, 32, 128, 512], P(None, 'row', 'col', 'gz')
- surface_flux: float32 [128, 1024], P('gz', ('row', 'col'))
Inputs may be any that keep to these rules, and one draw needn't show every extreme that they name: `trace_cell`: within each device's 1024 entries, entry values are local cell numbers, one from each aligned run of 8 consecutive cells, in a permuted order; the first and last cells of the block are always chosen. `flux_cell`: within each device's 4 entries, entry values are local cell numbers, one from each aligned run of 2048 consecutive cells, in a permuted order; the first and last cells of the block are always chosen.
All inputs are finite; a program needn't handle non-finite values.
Results may differ from a plain program's by a relative error of at most 0.0032.
Values may be sent and summed in bfloat16 or wider, within the bound.
A program may use at most 128 MiB of HBM per device.

v0:
```python
import jax
import jax.numpy as jnp
from jax import lax
from jax.sharding import PartitionSpec as P

OMEGA = 0.8


def padded_2(array, sides, width):
    for axis, dim in sides:
        peers, length = (lax.axis_size(axis), array.shape[dim])
        up = [(i, (i + 1) % peers) for i in range(peers - 1)]
        down = [(j, i) for i, j in up]
        last = lax.slice_in_dim(array, length - width, length, axis=dim)
        first = lax.slice_in_dim(array, 0, width, axis=dim)
        before = lax.ppermute(last, axis, up)
        after = lax.ppermute(first, axis, down)
        array = jnp.concatenate([before, array, after], axis=dim)
    return array


def relax(current, source, diagonal):
    padded = padded_2(current, (("row", 1), ("col", 2), ("gz", 3)), 1).astype(jnp.float32)
    centre = current.astype(jnp.float32)
    beside = padded[:, 2:, 1:-1, 1:-1] + padded[:, :-2, 1:-1, 1:-1]
    beside = beside + padded[:, 1:-1, 2:, 1:-1] + padded[:, 1:-1, :-2, 1:-1]
    beside = beside + padded[:, 1:-1, 1:-1, 2:] + padded[:, 1:-1, 1:-1, :-2]
    return (centre + OMEGA * (source - (diagonal * centre - beside)) / diagonal).astype(
        jnp.bfloat16
    )


def per_device(volume_field, volume_load, coefficient, surface_block, trace_cell, flux_cell):
    side_count, first_span, second_span, third_span = volume_field.shape
    cell_count = first_span * second_span * third_span
    slot_count = trace_cell.shape[3]
    flux_slots = flux_cell.shape[3]
    side_group = side_count // lax.axis_size("gz")
    flat_field = volume_field.reshape(side_count, cell_count)
    picker = (
        lax.broadcasted_iota(jnp.int32, (cell_count, slot_count), 0)
        == trace_cell.reshape(1, slot_count)
    ).astype(jnp.bfloat16)
    trace_values = jnp.dot(flat_field, picker, preferred_element_type=jnp.float32).astype(
        jnp.bfloat16
    )
    layer_index = lax.axis_index("gz")
    chosen = lax.dynamic_slice_in_dim(
        lax.all_gather(trace_values, ("row", "gz"), axis=1, tiled=True),
        layer_index * side_group,
        side_group,
        0,
    )
    partial_flux = lax.dot_general(
        chosen, surface_block, (((1,), (1,)), ((), ())), preferred_element_type=jnp.float32
    )
    surface_flux = lax.psum_scatter(partial_flux, "col", scatter_dimension=1, tiled=True)
    owned_flux = lax.all_to_all(surface_flux, "gz", split_axis=1, concat_axis=0, tiled=True)
    placer = (
        flux_cell.reshape(flux_slots, 1)
        == lax.broadcasted_iota(jnp.int32, (flux_slots, cell_count), 1)
    ).astype(jnp.float32)
    placed = jnp.dot(
        owned_flux, placer, precision=lax.Precision.HIGHEST, preferred_element_type=jnp.float32
    )
    source = volume_load.astype(jnp.float32) + placed.reshape(
        side_count, first_span, second_span, third_span
    )
    diagonal = 6.0 + coefficient
    current = volume_field
    for repeat in range(3):
        current = relax(current, source, diagonal)
    return (current, surface_flux)


def solution(mesh):
    in_specs = (
        P(None, "row", "col", "gz"),
        P(None, "row", "col", "gz"),
        P("row", "col", "gz"),
        P("row", "col"),
        P("row", "col", "gz", None),
        P("row", "col", "gz", None),
    )
    out_specs = (P(None, "row", "col", "gz"), P("gz", ("row", "col")))
    return jax.shard_map(
        per_device, mesh=mesh, in_specs=in_specs, out_specs=out_specs, check_vma=False
    )
```

profile of v0, /device:TPU:17, one launch (start us, length us, event | category | flops | bytes accessed | tf_op | source)
XLA Modules:
  0.0 316.4 jit_solution(1257853080280869536)
XLA Ops:
  7.2 8.3 %fusion.22 = bf16[128,1024]{1,0:T(8,128)(2,1)} fusion(bf16[16,8,64,128]{3,2,1,0:T(8,128)(2,1)} %bitcast.27, s32[1024]{0:T(1024)} %bitcast.29), kind=kOutput, calls=%fused_computation.46 | convolution fusion | flops 2156003328 | bytes 2363392 | tf_op jit(solution)/shard_map/dot_general | solution.py:44
  15.6 3.3 %copy.15 = bf16[128,8,8,128]{0,3,2,1:T(8,128)(2,1)S(1)} copy(bf16[128,8,8,128]{3,2,1,0:T(8,128)(2,1)} %param.6) | data formatting | bytes 4194304 | tf_op args[0]
  19.0 3.1 collective-permute-start
  23.4 3.7 %collective-permute-done = bf16[128,1,8,128]{0,3,2,1:T(8,128)(2,1)S(1)} collective-permute-done((bf16[128,1,8,128]{0,3,2,1:T(8,128)(2,1)S(1)}, bf16[128,1,8,128]{0,3,2,1:T(8,128)(2,1)S(1)}, u32[]{:S(2)}, u32[]{:S(2)}) %collective-permute-start) | collective-permute-done | bytes 262176 | tf_op jit(solution)/shard_map/ppermute | solution.py:16
  27.1 3.8 %collective-permute-done.1 = bf16[128,1,8,128]{0,3,2,1:T(8,128)(2,1)S(1)} collective-permute-done((bf16[128,1,8,128]{0,3,2,1:T(8,128)(2,1)S(1)}, bf16[128,1,8,128]{0,3,2,1:T(8,128)(2,1)S(1)}, u32[]{:S(2)}, u32[]{:S(2)}) %collective-permute-start.1) | collective-permute-done | bytes 262176 | tf_op jit(solution)/shard_map/ppermute | solution.py:17
  31.8 3.5 %collective-permute-start.2 = (bf16[128,10,1,128]{0,3,2,1:T(8,128)(2,1)}, bf16[128,10,1,128]{0,3,2,1:T(8,128)(2,1)S(1)}, u32[]{:S(2)}, u32[]{:S(2)}) collective-permute-start(bf16[128,10,1,128]{0,3,2,1:T(8,128)(2,1)} %get-tuple-element.16), channel_id=1, source_target_pairs={{0,4},{4,8},{8,12},{12,16},{16,20},{20,24},{24,28},{28,32},{32,36}... | collective-permute-start | bytes 983048 | tf_op jit(solution)/shard_map/ppermute | solution.py:16
  35.4 4.5 %collective-permute-start.3 = (bf16[128,10,1,128]{0,3,2,1:T(8,128)(2,1)}, bf16[128,10,1,128]{0,3,2,1:T(8,128)(2,1)S(1)}, u32[]{:S(2)}, u32[]{:S(2)}) collective-permute-start(bf16[128,10,1,128]{0,3,2,1:T(8,128)(2,1)} %get-tuple-element.17), channel_id=1, source_target_pairs={{4,0},{8,4},{12,8},{16,12},{20,16},{24,20},{28,24},{32,28},{36,32}... | collective-permute-start | bytes 983048 | tf_op jit(solution)/shard_map/ppermute | solution.py:17
  39.9 8.5 %collective-permute-done.2 = bf16[128,10,1,128]{0,3,2,1:T(8,128)(2,1)S(1)} collective-permute-done((bf16[128,10,1,128]{0,3,2,1:T(8,128)(2,1)}, bf16[128,10,1,128]{0,3,2,1:T(8,128)(2,1)S(1)}, u32[]{:S(2)}, u32[]{:S(2)}) %collective-permute-start.2) | collective-permute-done | bytes 327712 | tf_op jit(solution)/shard_map/ppermute | solution.py:16
  48.5 5.0 %collective-permute-done.3 = bf16[128,10,1,128]{0,3,2,1:T(8,128)(2,1)S(1)} collective-permute-done((bf16[128,10,1,128]{0,3,2,1:T(8,128)(2,1)}, bf16[128,10,1,128]{0,3,2,1:T(8,128)(2,1)S(1)}, u32[]{:S(2)}, u32[]{:S(2)}) %collective-permute-start.3) | collective-permute-done | bytes 327712 | tf_op jit(solution)/shard_map/ppermute | solution.py:17
  53.6 8.9 %collective-permute-start.4 = (bf16[128,10,10,1]{0,3,2,1:T(2,128)(2,1)S(1)}, bf16[128,10,10,1]{0,3,2,1:T(2,128)(2,1)S(1)}, u32[]{:S(2)}, u32[]{:S(2)}) collective-permute-start(bf16[128,10,10,1]{0,3,2,1:T(2,128)(2,1)S(1)} %get-tuple-element.10), channel_id=1, source_target_pairs={{0,1},{1,2},{2,3},{4,5},{5,6},{6,7},{8,9},{9,10},{10,11},{12,13},{... | collective-permute-start | bytes 76808 | tf_op jit(solution)/shard_map/ppermute | solution.py:16
  64.4 32.9 %all-gather.2.cloned.1.call-done = bf16[128,16384]{1,0:T(8,128)(2,1)} async-done(((bf16[128,1024]{1,0:T(8,128)(2,1)}), bf16[128,16384]{1,0:T(8,128)(2,1)}) %all-gather.2.cloned.1.call-update) | async-done | bytes 4194320 | tf_op jit(solution)/shard_map/all_gather | solution.py:49
  97.4 6.7 %fusion.25 = f32[32,256]{0,1:T(8,128)} fusion(bf16[256,16384]{1,0:T(8,128)(2,1)} %param.9, bf16[128,16384]{1,0:T(8,128)(2,1)} %all-gather.2.cloned.1.call-done, s32[]{:T(128)S(6)} %select_n.3), kind=kOutput, calls=%fused_computation.47 | convolution fusion | flops 268435456 | bytes 9469956 | tf_op jit(solution)/shard_map/dot_general | solution.py:54
  104.1 4.2 %copy.16 = bf16[128,8,8,128]{0,3,2,1:T(8,128)(2,1)} copy(bf16[128,8,8,128]{3,2,1,0:T(8,128)(2,1)} %param.7) | data formatting | bytes 4194304 | tf_op args[1]
  108.3 53.4 %reduce-scatter.2.cloned.1.call-done = f32[32,16]{0,1:T(8,128)} async-done(((f32[32,256]{0,1:T(8,128)}), f32[32,16]{0,1:T(8,128)}) %reduce-scatter.2.cloned.1.call-update) | async-done | bytes 2064 | tf_op jit(solution)/shard_map/reduce_scatter | solution.py:57
  163.1 17.1 %all-to-all-start = ((f32[4,1,128]{2,1,0:T(1,128)}), f32[4,1,128]{2,1,0:T(1,128)}, u32[]{:S(2)}, u32[]{:S(2)}) async-start(f32[4,1,128]{2,1,0:T(1,128)} %reshape.41), calls=%async_computation.1 | async-start | bytes 4096 | tf_op jit(solution)/shard_map/all_to_all | solution.py:58
  180.1 4.7 %maximum_convert_fusion = f32[128,10,10,130]{0,3,2,1:T(8,128)} fusion(bf16[128,10,10,1]{0,3,2,1:T(2,128)(2,1)S(1)} %collective-permute-done.5, bf16[128,10,1,128]{0,3,2,1:T(8,128)(2,1)S(1)} %collective-permute-done.3, bf16[128,1,8,128]{0,3,2,1:T(8,128)(2,1)S(1)} %collective-permute-done.1, bf16[128,8,8,128]{0,3,2,1:T(8,128)(2,1)S(1)} %copy.15, ...), kind=kLoop, calls=%fused_computation.40 | loop fusion | flops 23296000 | bytes 9984000 | tf_op jit(solution)/shard_map/convert_element_type | solution.py:23
  188.8 14.0 %fusion.14 = (bf16[128,8,8,128]{0,3,2,1:T(8,128)(2,1)S(1)}, f32[128,8,8,128]{0,3,2,1:T(8,128)}) fusion(f32[128,10,10,130]{0,3,2,1:T(8,128)} %maximum_convert_fusion, bf16[128,8,8,128]{0,3,2,1:T(8,128)(2,1)S(1)} %copy.15, f32[8,8,128]{2,1,0:T(8,128)S(1)} %broadcast_add_fusion, s32[8,8,128]{2,1,0:T(8,128)S(1)} %multiply_add_fusion, s32[4]{0:T(128)S(1)} %bitcast.30, ...), kind=kOutput, calls=%fused_computation.37 | convolution fusion | flops 66093056 | bytes 35719184 | tf_op jit(solution)/shard_map/dot_general | solution.py:63
  207.1 3.3 %collective-permute-done.6 = bf16[128,1,8,128]{0,3,2,1:T(8,128)(2,1)S(1)} collective-permute-done((bf16[128,1,8,128]{0,3,2,1:T(8,128)(2,1)S(1)}, bf16[128,1,8,128]{0,3,2,1:T(8,128)(2,1)S(1)}, u32[]{:S(2)}, u32[]{:S(2)}) %collective-permute-start.6) | collective-permute-done | bytes 262176 | tf_op jit(solution)/shard_map/ppermute | solution.py:16
  210.4 3.8 %collective-permute-done.7 = bf16[128,1,8,128]{0,3,2,1:T(8,128)(2,1)S(1)} collective-permute-done((bf16[128,1,8,128]{0,3,2,1:T(8,128)(2,1)S(1)}, bf16[128,1,8,128]{0,3,2,1:T(8,128)(2,1)S(1)}, u32[]{:S(2)}, u32[]{:S(2)}) %collective-permute-start.7) | collective-permute-done | bytes 262176 | tf_op jit(solution)/shard_map/ppermute | solution.py:17
  217.2 5.1 %collective-permute-start.9 = (bf16[128,10,1,128]{0,3,2,1:T(8,128)(2,1)S(1)}, bf16[128,10,1,128]{0,3,2,1:T(8,128)(2,1)S(1)}, u32[]{:S(2)}, u32[]{:S(2)}) collective-permute-start(bf16[128,10,1,128]{0,3,2,1:T(8,128)(2,1)S(1)} %get-tuple-element.15), channel_id=1, source_target_pairs={{4,0},{8,4},{12,8},{16,12},{20,16},{24,20},{28,24},{32,28},{36,32}... | collective-permute-start | bytes 983048 | tf_op jit(solution)/shard_map/ppermute | solution.py:17
  222.4 3.8 %collective-permute-done.8 = bf16[128,10,1,128]{0,3,2,1:T(8,128)(2,1)S(1)} collective-permute-done((bf16[128,10,1,128]{0,3,2,1:T(8,128)(2,1)S(1)}, bf16[128,10,1,128]{0,3,2,1:T(8,128)(2,1)S(1)}, u32[]{:S(2)}, u32[]{:S(2)}) %collective-permute-start.8) | collective-permute-done | bytes 327712 | tf_op jit(solution)/shard_map/ppermute | solution.py:16
  226.1 6.6 %collective-permute-done.9 = bf16[128,10,1,128]{0,3,2,1:T(8,128)(2,1)S(1)} collective-permute-done((bf16[128,10,1,128]{0,3,2,1:T(8,128)(2,1)S(1)}, bf16[128,10,1,128]{0,3,2,1:T(8,128)(2,1)S(1)}, u32[]{:S(2)}, u32[]{:S(2)}) %collective-permute-start.9) | collective-permute-done | bytes 327712 | tf_op jit(solution)/shard_map/ppermute | solution.py:17
  232.8 9.6 %collective-permute-start.10 = (bf16[128,10,10,1]{0,3,2,1:T(2,128)(2,1)S(1)}, bf16[128,10,10,1]{0,3,2,1:T(2,128)(2,1)S(1)}, u32[]{:S(2)}, u32[]{:S(2)}) collective-permute-start(bf16[128,10,10,1]{0,3,2,1:T(2,128)(2,1)S(1)} %get-tuple-element.8), channel_id=1, source_target_pairs={{0,1},{1,2},{2,3},{4,5},{5,6},{6,7},{8,9},{9,10},{10,11},{12,13},{... | collective-permute-start | bytes 76808 | tf_op jit(solution)/shard_map/ppermute | solution.py:16
  244.7 7.4 %collective-permute-done.11 = bf16[128,10,10,1]{0,3,2,1:T(2,128)(2,1)S(1)} collective-permute-done((bf16[128,10,10,1]{0,3,2,1:T(2,128)(2,1)S(1)}, bf16[128,10,10,1]{0,3,2,1:T(2,128)(2,1)S(1)}, u32[]{:S(2)}, u32[]{:S(2)}) %collective-permute-start.11) | collective-permute-done | bytes 25632 | tf_op jit(solution)/shard_map/ppermute | solution.py:17
  255.1 4.5 %fusion.15 = bf16[128,8,8,128]{0,3,2,1:T(8,128)(2,1)S(1)} fusion(f32[128,8,8,128]{0,3,2,1:T(8,128)S(1)} %copy-done, f32[128,10,10,130]{0,3,2,1:T(8,128)S(1)} %maximum_convert_fusion.1, bf16[128,8,8,128]{0,3,2,1:T(8,128)(2,1)S(1)} %get-tuple-element.24, f32[8,8,128]{2,1,0:T(8,128)S(1)} %broadcast_add_fusion), kind=kLoop, calls=%fused_computation.38 | loop fusion | flops 13631488 | bytes 33587200 | tf_op jit(solution)/shard_map/convert_element_type | solution.py:28
  266.0 3.8 %collective-permute-done.13 = bf16[128,1,8,128]{0,3,2,1:T(8,128)(2,1)S(1)} collective-permute-done((bf16[128,1,8,128]{0,3,2,1:T(8,128)(2,1)S(1)}, bf16[128,1,8,128]{0,3,2,1:T(8,128)(2,1)S(1)}, u32[]{:S(2)}, u32[]{:S(2)}) %collective-permute-start.13) | collective-permute-done | bytes 262176 | tf_op jit(solution)/shard_map/ppermute | solution.py:17
  270.0 4.6 %collective-permute-start.14 = (bf16[128,10,1,128]{0,3,2,1:T(8,128)(2,1)S(1)}, bf16[128,10,1,128]{0,3,2,1:T(8,128)(2,1)S(1)}, u32[]{:S(2)}, u32[]{:S(2)}) collective-permute-start(bf16[128,10,1,128]{0,3,2,1:T(8,128)(2,1)S(1)} %get-tuple-element.12), channel_id=1, source_target_pairs={{0,4},{4,8},{8,12},{12,16},{16,20},{20,24},{24,28},{28,32},{32,36}... | collective-permute-start | bytes 983048 | tf_op jit(solution)/shard_map/ppermute | solution.py:16
  274.5 3.4 %collective-permute-start.15 = (bf16[128,10,1,128]{0,3,2,1:T(8,128)(2,1)S(1)}, bf16[128,10,1,128]{0,3,2,1:T(8,128)(2,1)S(1)}, u32[]{:S(2)}, u32[]{:S(2)}) collective-permute-start(bf16[128,10,1,128]{0,3,2,1:T(8,128)(2,1)S(1)} %get-tuple-element.13), channel_id=1, source_target_pairs={{4,0},{8,4},{12,8},{16,12},{20,16},{24,20},{28,24},{32,28},{36,32}... | collective-permute-start | bytes 983048 | tf_op jit(solution)/shard_map/ppermute | solution.py:17
  278.0 5.4 %collective-permute-done.14 = bf16[128,10,1,128]{0,3,2,1:T(8,128)(2,1)S(1)} collective-permute-done((bf16[128,10,1,128]{0,3,2,1:T(8,128)(2,1)S(1)}, bf16[128,10,1,128]{0,3,2,1:T(8,128)(2,1)S(1)}, u32[]{:S(2)}, u32[]{:S(2)}) %collective-permute-start.14) | collective-permute-done | bytes 327712 | tf_op jit(solution)/shard_map/ppermute | solution.py:16
  283.3 4.6 %collective-permute-done.15 = bf16[128,10,1,128]{0,3,2,1:T(8,128)(2,1)S(1)} collective-permute-done((bf16[128,10,1,128]{0,3,2,1:T(8,128)(2,1)S(1)}, bf16[128,10,1,128]{0,3,2,1:T(8,128)(2,1)S(1)}, u32[]{:S(2)}, u32[]{:S(2)}) %collective-permute-start.15) | collective-permute-done | bytes 327712 | tf_op jit(solution)/shard_map/ppermute | solution.py:17
  292.3 6.9 %collective-permute-done.17 = bf16[128,10,10,1]{0,3,2,1:T(2,128)(2,1)S(1)} collective-permute-done((bf16[128,10,10,1]{0,3,2,1:T(2,128)(2,1)S(1)}, bf16[128,10,10,1]{0,3,2,1:T(2,128)(2,1)S(1)}, u32[]{:S(2)}, u32[]{:S(2)}) %collective-permute-start.17) | collective-permute-done | bytes 25632 | tf_op jit(solution)/shard_map/ppermute | solution.py:17
  302.2 4.5 %fusion.16 = bf16[128,8,8,128]{0,3,2,1:T(8,128)(2,1)S(1)} fusion(f32[128,8,8,128]{0,3,2,1:T(8,128)S(1)} %copy-done, f32[128,10,10,130]{0,3,2,1:T(8,128)S(1)} %maximum_convert_fusion.2, bf16[128,8,8,128]{0,3,2,1:T(8,128)(2,1)S(1)} %fusion.15, f32[8,8,128]{2,1,0:T(8,128)S(1)} %broadcast_add_fusion), kind=kLoop, calls=%fused_computation.39 | loop fusion | flops 13631488 | bytes 33587200 | tf_op jit(solution)/shard_map/convert_element_type | solution.py:28
  (47 shorter events, 38.8 us)
Async XLA Ops:
  7.2 90.2 %all-gather.2.cloned.1.call-start = ((), (), s32[]{:S(2)}) async-start(), calls=%async_computation.2 | async-start | bytes 4456448 | tf_op jit(solution)/shard_map/all_gather | solution.py:49
  15.5 24.4 %copy-start.1 = (f32[8,8,128]{2,1,0:T(8,128)S(1)}, f32[8,8,128]{2,1,0:T(8,128)}, u32[]{:S(2)}) copy-start(f32[8,8,128]{2,1,0:T(8,128)} %param.8) | copy-start | bytes 98308
  15.6 146.1 %reduce-scatter.2.cloned.1.call-start = ((), (), s32[]{:S(2)}) async-start(), calls=%async_computation.3 | async-start | bytes 139264 | tf_op jit(solution)/shard_map/reduce_scatter | solution.py:57
  19.0 8.1 %collective-permute-start = (bf16[128,1,8,128]{0,3,2,1:T(8,128)(2,1)S(1)}, bf16[128,1,8,128]{0,3,2,1:T(8,128)(2,1)S(1)}, u32[]{:S(2)}, u32[]{:S(2)}) collective-permute-start(bf16[128,1,8,128]{0,3,2,1:T(8,128)(2,1)S(1)} %get-tuple-element.22), channel_id=1, source_target_pairs={{0,64},{64,128},{128,192},{1,65},{65,129},{129,193},{2,66},{66,130... | collective-permute-start | bytes 786440 | tf_op jit(solution)/shard_map/ppermute | solution.py:16
  22.1 8.8 %collective-permute-start.1 = (bf16[128,1,8,128]{0,3,2,1:T(8,128)(2,1)S(1)}, bf16[128,1,8,128]{0,3,2,1:T(8,128)(2,1)S(1)}, u32[]{:S(2)}, u32[]{:S(2)}) collective-permute-start(bf16[128,1,8,128]{0,3,2,1:T(8,128)(2,1)S(1)} %get-tuple-element.23), channel_id=1, source_target_pairs={{64,0},{128,64},{192,128},{65,1},{129,65},{193,129},{66,2},{130,66... | collective-permute-start | bytes 786440 | tf_op jit(solution)/shard_map/ppermute | solution.py:17
  31.8 16.6 %collective-permute-start.2 = (bf16[128,10,1,128]{0,3,2,1:T(8,128)(2,1)}, bf16[128,10,1,128]{0,3,2,1:T(8,128)(2,1)S(1)}, u32[]{:S(2)}, u32[]{:S(2)}) collective-permute-start(bf16[128,10,1,128]{0,3,2,1:T(8,128)(2,1)} %get-tuple-element.16), channel_id=1, source_target_pairs={{0,4},{4,8},{8,12},{12,16},{16,20},{20,24},{24,28},{28,32},{32,36}... | collective-permute-start | bytes 983048 | tf_op jit(solution)/shard_map/ppermute | solution.py:16
  35.4 18.1 %collective-permute-start.3 = (bf16[128,10,1,128]{0,3,2,1:T(8,128)(2,1)}, bf16[128,10,1,128]{0,3,2,1:T(8,128)(2,1)S(1)}, u32[]{:S(2)}, u32[]{:S(2)}) collective-permute-start(bf16[128,10,1,128]{0,3,2,1:T(8,128)(2,1)} %get-tuple-element.17), channel_id=1, source_target_pairs={{4,0},{8,4},{12,8},{16,12},{20,16},{24,20},{28,24},{32,28},{36,32}... | collective-permute-start | bytes 983048 | tf_op jit(solution)/shard_map/ppermute | solution.py:17
  53.6 126.6 %collective-permute-start.4 = (bf16[128,10,10,1]{0,3,2,1:T(2,128)(2,1)S(1)}, bf16[128,10,10,1]{0,3,2,1:T(2,128)(2,1)S(1)}, u32[]{:S(2)}, u32[]{:S(2)}) collective-permute-start(bf16[128,10,10,1]{0,3,2,1:T(2,128)(2,1)S(1)} %get-tuple-element.10), channel_id=1, source_target_pairs={{0,1},{1,2},{2,3},{4,5},{5,6},{6,7},{8,9},{9,10},{10,11},{12,13},{... | collective-permute-start | bytes 76808 | tf_op jit(solution)/shard_map/ppermute | solution.py:16
  62.5 117.6 %collective-permute-start.5 = (bf16[128,10,10,1]{0,3,2,1:T(2,128)(2,1)S(1)}, bf16[128,10,10,1]{0,3,2,1:T(2,128)(2,1)S(1)}, u32[]{:S(2)}, u32[]{:S(2)}) collective-permute-start(bf16[128,10,10,1]{0,3,2,1:T(2,128)(2,1)S(1)} %get-tuple-element.11), channel_id=1, source_target_pairs={{1,0},{2,1},{3,2},{5,4},{6,5},{7,6},{9,8},{10,9},{11,10},{13,12},{... | collective-permute-start | bytes 76808 | tf_op jit(solution)/shard_map/ppermute | solution.py:17
  163.1 23.9 %all-to-all-start = ((f32[4,1,128]{2,1,0:T(1,128)}), f32[4,1,128]{2,1,0:T(1,128)}, u32[]{:S(2)}, u32[]{:S(2)}) async-start(f32[4,1,128]{2,1,0:T(1,128)} %reshape.41), calls=%async_computation.1 | async-start | bytes 4096 | tf_op jit(solution)/shard_map/all_to_all | solution.py:58
  180.1 8.7 %copy-start.2 = (s32[1,1,1,4]{3,2,1,0:T(1,128)S(1)}, s32[1,1,1,4]{3,2,1,0:T(1,128)}, u32[]{:S(2)}) copy-start(s32[1,1,1,4]{3,2,1,0:T(1,128)} %param.11) | copy-start | bytes 52
  202.8 7.6 %collective-permute-start.6 = (bf16[128,1,8,128]{0,3,2,1:T(8,128)(2,1)S(1)}, bf16[128,1,8,128]{0,3,2,1:T(8,128)(2,1)S(1)}, u32[]{:S(2)}, u32[]{:S(2)}) collective-permute-start(bf16[128,1,8,128]{0,3,2,1:T(8,128)(2,1)S(1)} %get-tuple-element.20), channel_id=1, source_target_pairs={{0,64},{64,128},{128,192},{1,65},{65,129},{129,193},{2,66},{66,130... | collective-permute-start | bytes 786440 | tf_op jit(solution)/shard_map/ppermute | solution.py:16
  205.8 8.5 %collective-permute-start.7 = (bf16[128,1,8,128]{0,3,2,1:T(8,128)(2,1)S(1)}, bf16[128,1,8,128]{0,3,2,1:T(8,128)(2,1)S(1)}, u32[]{:S(2)}, u32[]{:S(2)}) collective-permute-start(bf16[128,1,8,128]{0,3,2,1:T(8,128)(2,1)S(1)} %get-tuple-element.21), channel_id=1, source_target_pairs={{64,0},{128,64},{192,128},{65,1},{129,65},{193,129},{66,2},{130,66... | collective-permute-start | bytes 786440 | tf_op jit(solution)/shard_map/ppermute | solution.py:17
  214.4 11.8 %collective-permute-start.8 = (bf16[128,10,1,128]{0,3,2,1:T(8,128)(2,1)S(1)}, bf16[128,10,1,128]{0,3,2,1:T(8,128)(2,1)S(1)}, u32[]{:S(2)}, u32[]{:S(2)}) collective-permute-start(bf16[128,10,1,128]{0,3,2,1:T(8,128)(2,1)S(1)} %get-tuple-element.14), channel_id=1, source_target_pairs={{0,4},{4,8},{8,12},{12,16},{16,20},{20,24},{24,28},{28,32},{32,36}... | collective-permute-start | bytes 983048 | tf_op jit(solution)/shard_map/ppermute | solution.py:16
  217.2 15.5 %collective-permute-start.9 = (bf16[128,10,1,128]{0,3,2,1:T(8,128)(2,1)S(1)}, bf16[128,10,1,128]{0,3,2,1:T(8,128)(2,1)S(1)}, u32[]{:S(2)}, u32[]{:S(2)}) collective-permute-start(bf16[128,10,1,128]{0,3,2,1:T(8,128)(2,1)S(1)} %get-tuple-element.15), channel_id=1, source_target_pairs={{4,0},{8,4},{12,8},{16,12},{20,16},{24,20},{28,24},{32,28},{36,32}... | collective-permute-start | bytes 983048 | tf_op jit(solution)/shard_map/ppermute | solution.py:17
  232.8 11.9 %collective-permute-start.10 = (bf16[128,10,10,1]{0,3,2,1:T(2,128)(2,1)S(1)}, bf16[128,10,10,1]{0,3,2,1:T(2,128)(2,1)S(1)}, u32[]{:S(2)}, u32[]{:S(2)}) collective-permute-start(bf16[128,10,10,1]{0,3,2,1:T(2,128)(2,1)S(1)} %get-tuple-element.8), channel_id=1, source_target_pairs={{0,1},{1,2},{2,3},{4,5},{5,6},{6,7},{8,9},{9,10},{10,11},{12,13},{... | collective-permute-start | bytes 76808 | tf_op jit(solution)/shard_map/ppermute | solution.py:16
  242.5 12.6 %copy-start = (f32[128,8,8,128]{0,3,2,1:T(8,128)S(1)}, f32[128,8,8,128]{0,3,2,1:T(8,128)}, u32[]{:S(2)}) copy-start(f32[128,8,8,128]{0,3,2,1:T(8,128)} %get-tuple-element.25) | copy-start | bytes 12582916
  242.5 9.6 %collective-permute-start.11 = (bf16[128,10,10,1]{0,3,2,1:T(2,128)(2,1)S(1)}, bf16[128,10,10,1]{0,3,2,1:T(2,128)(2,1)S(1)}, u32[]{:S(2)}, u32[]{:S(2)}) collective-permute-start(bf16[128,10,10,1]{0,3,2,1:T(2,128)(2,1)S(1)} %get-tuple-element.9), channel_id=1, source_target_pairs={{1,0},{2,1},{3,2},{5,4},{6,5},{7,6},{9,8},{10,9},{11,10},{13,12},{... | collective-permute-start | bytes 76808 | tf_op jit(solution)/shard_map/ppermute | solution.py:17
  259.7 6.4 %collective-permute-start.12 = (bf16[128,1,8,128]{0,3,2,1:T(8,128)(2,1)S(1)}, bf16[128,1,8,128]{0,3,2,1:T(8,128)(2,1)S(1)}, u32[]{:S(2)}, u32[]{:S(2)}) collective-permute-start(bf16[128,1,8,128]{0,3,2,1:T(8,128)(2,1)S(1)} %get-tuple-element.18), channel_id=1, source_target_pairs={{0,64},{64,128},{128,192},{1,65},{65,129},{129,193},{2,66},{66,130... | collective-permute-start | bytes 786440 | tf_op jit(solution)/shard_map/ppermute | solution.py:16
  262.8 7.1 %collective-permute-start.13 = (bf16[128,1,8,128]{0,3,2,1:T(8,128)(2,1)S(1)}, bf16[128,1,8,128]{0,3,2,1:T(8,128)(2,1)S(1)}, u32[]{:S(2)}, u32[]{:S(2)}) collective-permute-start(bf16[128,1,8,128]{0,3,2,1:T(8,128)(2,1)S(1)} %get-tuple-element.19), channel_id=1, source_target_pairs={{64,0},{128,64},{192,128},{65,1},{129,65},{193,129},{66,2},{130,66... | collective-permute-start | bytes 786440 | tf_op jit(solution)/shard_map/ppermute | solution.py:17
  270.0 13.4 %collective-permute-start.14 = (bf16[128,10,1,128]{0,3,2,1:T(8,128)(2,1)S(1)}, bf16[128,10,1,128]{0,3,2,1:T(8,128)(2,1)S(1)}, u32[]{:S(2)}, u32[]{:S(2)}) collective-permute-start(bf16[128,10,1,128]{0,3,2,1:T(8,128)(2,1)S(1)} %get-tuple-element.12), channel_id=1, source_target_pairs={{0,4},{4,8},{8,12},{12,16},{16,20},{20,24},{24,28},{28,32},{32,36}... | collective-permute-start | bytes 983048 | tf_op jit(solution)/shard_map/ppermute | solution.py:16
  274.5 13.4 %collective-permute-start.15 = (bf16[128,10,1,128]{0,3,2,1:T(8,128)(2,1)S(1)}, bf16[128,10,1,128]{0,3,2,1:T(8,128)(2,1)S(1)}, u32[]{:S(2)}, u32[]{:S(2)}) collective-permute-start(bf16[128,10,1,128]{0,3,2,1:T(8,128)(2,1)S(1)} %get-tuple-element.13), channel_id=1, source_target_pairs={{4,0},{8,4},{12,8},{16,12},{20,16},{24,20},{28,24},{32,28},{36,32}... | collective-permute-start | bytes 983048 | tf_op jit(solution)/shard_map/ppermute | solution.py:17
  288.0 4.3 %collective-permute-start.16 = (bf16[128,10,10,1]{0,3,2,1:T(2,128)(2,1)S(1)}, bf16[128,10,10,1]{0,3,2,1:T(2,128)(2,1)S(1)}, u32[]{:S(2)}, u32[]{:S(2)}) collective-permute-start(bf16[128,10,10,1]{0,3,2,1:T(2,128)(2,1)S(1)} %get-tuple-element.6), channel_id=1, source_target_pairs={{0,1},{1,2},{2,3},{4,5},{5,6},{6,7},{8,9},{9,10},{10,11},{12,13},{... | collective-permute-start | bytes 76808 | tf_op jit(solution)/shard_map/ppermute | solution.py:16
  289.9 9.3 %collective-permute-start.17 = (bf16[128,10,10,1]{0,3,2,1:T(2,128)(2,1)S(1)}, bf16[128,10,10,1]{0,3,2,1:T(2,128)(2,1)S(1)}, u32[]{:S(2)}, u32[]{:S(2)}) collective-permute-start(bf16[128,10,10,1]{0,3,2,1:T(2,128)(2,1)S(1)} %get-tuple-element.7), channel_id=1, source_target_pairs={{1,0},{2,1},{3,2},{5,4},{6,5},{7,6},{9,8},{10,9},{11,10},{13,12},{... | collective-permute-start | bytes 76808 | tf_op jit(solution)/shard_map/ppermute | solution.py:17
Sparse Core Ops, SparseCore 0:
  15.7 81.6 all-gather.1
  104.2 57.4 reduce-scatter.1
where the time goes:
time: 317 us; the launch traced here: 316 us
  waiting for transfers between devices  157 us (50%)
  starting transfers between devices  81.2 us (26%)
  matrix products  28.9 us (9%)
  other arithmetic  22.3 us (7%)
  between operations  14.3 us (5%)
  local copies, waits for them, and re-layouts  12.4 us (4%)
    reduce_scatter x1, waiting for transfers between devices, per_device(): lax.psum_scatter(partial_flux, 'col', scatter_dimension=1, tiled=True)  53.4 us
    ppermute x9, waiting for transfers between devices, padded_2(): after = lax.ppermute(first, axis, down)  42 us
    ppermute x9, starting transfers between devices, padded_2(): before = lax.ppermute(last, axis, up)  40.6 us
    all_gather x1, waiting for transfers between devices, per_device(): lax.all_gather(trace_values, ('row', 'gz'), axis=1, tiled=True)  32.9 us
    ppermute x9, waiting for transfers between devices, padded_2(): before = lax.ppermute(last, axis, up)  26.7 us
    ppermute x9, starting transfers between devices, padded_2(): after = lax.ppermute(first, axis, down)  23.4 us
    all_to_all x1, starting transfers between devices, per_device(): lax.all_to_all(surface_flux, 'gz', split_axis=1, concat_axis=0, tiled=True)  17.1 us
    dot_general x1, matrix products, per_device(): jnp.dot(owned_flux, placer, precision=lax.Precision.HIGHEST, preferred_el...  14 us
  transfers between devices with their start and end apart: 21, of which 17 were waited for; matrix products, arithmetic and copies ran while one was open for 7% of the time, Pallas kernels for 0%

commit v1 on v0

--- a/solution.py
+++ b/solution.py
@@ -4,6 +4,13 @@
 from jax.sharding import PartitionSpec as P
 
 OMEGA = 0.8
+
+
+def swap_blocks(value, mesh_axis, split, join):
+    peers = lax.axis_size(mesh_axis)
+    parts = jnp.stack(jnp.split(value, peers, axis=split), axis=0)
+    parts = lax.all_to_all(parts, mesh_axis, split_axis=0, concat_axis=0)
+    return jnp.concatenate(parts, axis=join)
 
 
 def padded_2(array, sides, width):
@@ -55,7 +62,7 @@
         chosen, surface_block, (((1,), (1,)), ((), ())), preferred_element_type=jnp.float32
     )
     surface_flux = lax.psum_scatter(partial_flux, "col", scatter_dimension=1, tiled=True)
-    owned_flux = lax.all_to_all(surface_flux, "gz", split_axis=1, concat_axis=0, tiled=True)
+    owned_flux = swap_blocks(surface_flux, "gz", 1, 0)
     placer = (
         flux_cell.reshape(flux_slots, 1)
         == lax.broadcasted_iota(jnp.int32, (flux_slots, cell_count), 1)

time: 317 us -> 316 us (level)
  starting transfers between devices: 81.2 us -> 72.8 us
  waiting for transfers between devices: 157 us -> 164 us
    all_gather x1, waiting for transfers between devices: 32.9 us -> 56.3 us  [per_device(): lax.all_gather(trace_values, ('row', 'gz'), axis=1, tiled=True)]
    ppermute x9, waiting for transfers between devices: 26.7 us -> 15.4 us  [padded_2(): before = lax.ppermute(last, axis, up)]
    ppermute x9, starting transfers between devices: 40.6 us -> 31.7 us  [padded_2(): before = lax.ppermute(last, axis, up)]
    ppermute x9, waiting for transfers between devices: 42 us -> 36.6 us  [padded_2(): after = lax.ppermute(first, axis, down)]
    unnamed x11 -> x13, local copies, waits for them, and re-layouts: 11.7 us -> 11 us
  transfers between devices with their start and end apart: 21 -> 21, of which waited for: 17 -> 14; matrix products, arithmetic and copies ran while one was open for 7% -> 7% of each run, Pallas kernels for 0% -> 0%
where the time goes in v1:
time: 316 us
  waiting for transfers between devices  164 us (52%)
  starting transfers between devices  72.8 us (23%)
  matrix products  29 us (9%)
  other arithmetic  23.1 us (7%)
  between operations  14.4 us (5%)
  local copies, waits for them, and re-layouts  12.6 us (4%)
    all_gather x1, waiting for transfers between devices, per_device(): lax.all_gather(trace_values, ('row', 'gz'), axis=1, tiled=True)  56.3 us
    reduce_scatter x1, waiting for transfers between devices, per_device(): lax.psum_scatter(partial_flux, 'col', scatter_dimension=1, tiled=True)  53 us
    ppermute x9, waiting for transfers between devices, padded_2(): after = lax.ppermute(first, axis, down)  36.6 us
    ppermute x9, starting transfers between devices, padded_2(): before = lax.ppermute(last, axis, up)  31.7 us
    ppermute x9, starting transfers between devices, padded_2(): after = lax.ppermute(first, axis, down)  23.9 us
    all_to_all x1, starting transfers between devices, swap_blocks(): parts = lax.all_to_all(parts, mesh_axis, split_axis=0, concat_axis=0)  17.1 us
    ppermute x9, waiting for transfers between devices, padded_2(): before = lax.ppermute(last, axis, up)  15.4 us
    dot_general x1, matrix products, per_device(): jnp.dot(owned_flux, placer, precision=lax.Precision.HIGHEST, preferred_el...  14.1 us
  transfers between devices with their start and end apart: 21, of which 14 were waited for; matrix products, arithmetic and copies ran while one was open for 7% of the time, Pallas kernels for 0%

profile of v1, /device:TPU:17, one launch (start us, length us, event | category | flops | bytes accessed | tf_op | source)
XLA Modules:
  0.0 315.6 jit_solution(11658105600428926654)
XLA Ops:
  7.2 8.3 %fusion.22 = bf16[128,1024]{1,0:T(8,128)(2,1)} fusion(bf16[16,8,64,128]{3,2,1,0:T(8,128)(2,1)} %bitcast.32, s32[1024]{0:T(1024)} %bitcast.34), kind=kOutput, calls=%fused_computation.46 | convolution fusion | flops 2156003328 | bytes 2363392 | tf_op jit(solution)/shard_map/dot_general | solution.py:51
  15.6 3.3 %copy.15 = bf16[128,8,8,128]{0,3,2,1:T(8,128)(2,1)S(1)} copy(bf16[128,8,8,128]{3,2,1,0:T(8,128)(2,1)} %param.6) | data formatting | bytes 4194304 | tf_op args[0]
  19.0 3.1 collective-permute-start
  24.0 4.2 %copy.16 = bf16[128,8,8,128]{0,3,2,1:T(8,128)(2,1)} copy(bf16[128,8,8,128]{3,2,1,0:T(8,128)(2,1)} %param.7) | data formatting | bytes 4194304 | tf_op args[1]
  31.8 3.5 %collective-permute-start.2 = (bf16[128,10,1,128]{0,3,2,1:T(8,128)(2,1)}, bf16[128,10,1,128]{0,3,2,1:T(8,128)(2,1)S(1)}, u32[]{:S(2)}, u32[]{:S(2)}) collective-permute-start(bf16[128,10,1,128]{0,3,2,1:T(8,128)(2,1)} %get-tuple-element.16), channel_id=1, source_target_pairs={{0,4},{4,8},{8,12},{12,16},{16,20},{20,24},{24,28},{28,32},{32,36}... | collective-permute-start | bytes 983048 | tf_op jit(solution)/shard_map/ppermute | solution.py:23
  35.4 4.5 %collective-permute-start.3 = (bf16[128,10,1,128]{0,3,2,1:T(8,128)(2,1)}, bf16[128,10,1,128]{0,3,2,1:T(8,128)(2,1)S(1)}, u32[]{:S(2)}, u32[]{:S(2)}) collective-permute-start(bf16[128,10,1,128]{0,3,2,1:T(8,128)(2,1)} %get-tuple-element.17), channel_id=1, source_target_pairs={{4,0},{8,4},{12,8},{16,12},{20,16},{24,20},{28,24},{32,28},{36,32}... | collective-permute-start | bytes 983048 | tf_op jit(solution)/shard_map/ppermute | solution.py:24
  39.9 56.3 %all-gather.2.cloned.1.call-done = bf16[128,16384]{1,0:T(8,128)(2,1)} async-done(((bf16[128,1024]{1,0:T(8,128)(2,1)}), bf16[128,16384]{1,0:T(8,128)(2,1)}) %all-gather.2.cloned.1.call-update) | async-done | bytes 4194320 | tf_op jit(solution)/shard_map/all_gather | solution.py:56
  96.2 6.7 %fusion.25 = f32[32,256]{0,1:T(8,128)} fusion(bf16[256,16384]{1,0:T(8,128)(2,1)} %param.9, bf16[128,16384]{1,0:T(8,128)(2,1)} %all-gather.2.cloned.1.call-done, s32[]{:T(128)S(6)} %select_n.3), kind=kOutput, calls=%fused_computation.47 | convolution fusion | flops 268435456 | bytes 9469956 | tf_op jit(solution)/shard_map/dot_general | solution.py:61
  107.4 53.0 %reduce-scatter.2.cloned.1.call-done = f32[32,16]{0,1:T(8,128)} async-done(((f32[32,256]{0,1:T(8,128)}), f32[32,16]{0,1:T(8,128)}) %reduce-scatter.2.cloned.1.call-update) | async-done | bytes 2064 | tf_op jit(solution)/shard_map/reduce_scatter | solution.py:64
  161.8 17.1 %all-to-all-start = ((f32[4,1,128]{2,1,0:T(1,128)}), f32[4,1,128]{2,1,0:T(1,128)}, u32[]{:S(2)}, u32[]{:S(2)}) async-start(f32[4,1,128]{2,1,0:T(1,128)} %reshape.42), calls=%async_computation.1 | async-start | bytes 4096 | tf_op jit(solution)/shard_map/all_to_all | solution.py:12
  179.0 4.8 %maximum_convert_fusion = f32[128,10,10,130]{0,3,2,1:T(8,128)} fusion(bf16[128,10,10,1]{0,3,2,1:T(2,128)(2,1)S(1)} %collective-permute-done.5, bf16[128,10,1,128]{0,3,2,1:T(8,128)(2,1)S(1)} %collective-permute-done.3, bf16[128,1,8,128]{0,3,2,1:T(8,128)(2,1)S(1)} %collective-permute-done.1, bf16[128,8,8,128]{0,3,2,1:T(8,128)(2,1)S(1)} %copy.15, ...), kind=kLoop, calls=%fused_computation.40 | loop fusion | flops 23296000 | bytes 9984000 | tf_op jit(solution)/shard_map/convert_element_type | solution.py:30
  188.2 14.1 %fusion.14 = (bf16[128,8,8,128]{0,3,2,1:T(8,128)(2,1)S(1)}, f32[128,8,8,128]{0,3,2,1:T(8,128)}) fusion(f32[128,10,10,130]{0,3,2,1:T(8,128)} %maximum_convert_fusion, bf16[128,8,8,128]{0,3,2,1:T(8,128)(2,1)S(1)} %copy.15, f32[8,8,128]{2,1,0:T(8,128)S(1)} %broadcast_add_fusion, s32[8,8,128]{2,1,0:T(8,128)S(1)} %copy-done.2, s32[4]{0:T(128)S(1)} %bitcast.35, ...), kind=kOutput, calls=%fused_computation.37 | convolution fusion | flops 66093056 | bytes 35719184 | tf_op jit(solution)/shard_map/dot_general | solution.py:70
  202.3 3.1 collective-permute-start.6
  206.7 3.8 %collective-permute-done.6 = bf16[128,1,8,128]{0,3,2,1:T(8,128)(2,1)S(1)} collective-permute-done((bf16[128,1,8,128]{0,3,2,1:T(8,128)(2,1)S(1)}, bf16[128,1,8,128]{0,3,2,1:T(8,128)(2,1)S(1)}, u32[]{:S(2)}, u32[]{:S(2)}) %collective-permute-start.6) | collective-permute-done | bytes 262176 | tf_op jit(solution)/shard_map/ppermute | solution.py:23
  210.5 3.8 %collective-permute-done.7 = bf16[128,1,8,128]{0,3,2,1:T(8,128)(2,1)S(1)} collective-permute-done((bf16[128,1,8,128]{0,3,2,1:T(8,128)(2,1)S(1)}, bf16[128,1,8,128]{0,3,2,1:T(8,128)(2,1)S(1)}, u32[]{:S(2)}, u32[]{:S(2)}) %collective-permute-start.7) | collective-permute-done | bytes 262176 | tf_op jit(solution)/shard_map/ppermute | solution.py:24
  214.4 2.9 collective-permute-start.8
  217.3 5.1 %collective-permute-start.9 = (bf16[128,10,1,128]{0,3,2,1:T(8,128)(2,1)S(1)}, bf16[128,10,1,128]{0,3,2,1:T(8,128)(2,1)S(1)}, u32[]{:S(2)}, u32[]{:S(2)}) collective-permute-start(bf16[128,10,1,128]{0,3,2,1:T(8,128)(2,1)S(1)} %get-tuple-element.15), channel_id=1, source_target_pairs={{4,0},{8,4},{12,8},{16,12},{20,16},{24,20},{28,24},{32,28},{36,32}... | collective-permute-start | bytes 983048 | tf_op jit(solution)/shard_map/ppermute | solution.py:24
  222.4 4.2 %collective-permute-done.8 = bf16[128,10,1,128]{0,3,2,1:T(8,128)(2,1)S(1)} collective-permute-done((bf16[128,10,1,128]{0,3,2,1:T(8,128)(2,1)S(1)}, bf16[128,10,1,128]{0,3,2,1:T(8,128)(2,1)S(1)}, u32[]{:S(2)}, u32[]{:S(2)}) %collective-permute-start.8) | collective-permute-done | bytes 327712 | tf_op jit(solution)/shard_map/ppermute | solution.py:23
  226.7 7.3 %collective-permute-done.9 = bf16[128,10,1,128]{0,3,2,1:T(8,128)(2,1)S(1)} collective-permute-done((bf16[128,10,1,128]{0,3,2,1:T(8,128)(2,1)S(1)}, bf16[128,10,1,128]{0,3,2,1:T(8,128)(2,1)S(1)}, u32[]{:S(2)}, u32[]{:S(2)}) %collective-permute-start.9) | collective-permute-done | bytes 327712 | tf_op jit(solution)/shard_map/ppermute | solution.py:24
  234.1 7.6 %collective-permute-start.10 = (bf16[128,10,10,1]{0,3,2,1:T(2,128)(2,1)S(1)}, bf16[128,10,10,1]{0,3,2,1:T(2,128)(2,1)S(1)}, u32[]{:S(2)}, u32[]{:S(2)}) collective-permute-start(bf16[128,10,10,1]{0,3,2,1:T(2,128)(2,1)S(1)} %get-tuple-element.8), channel_id=1, source_target_pairs={{0,1},{1,2},{2,3},{4,5},{5,6},{6,7},{8,9},{9,10},{10,11},{12,13},{... | collective-permute-start | bytes 76808 | tf_op jit(solution)/shard_map/ppermute | solution.py:23
  243.9 7.4 %collective-permute-done.11 = bf16[128,10,10,1]{0,3,2,1:T(2,128)(2,1)S(1)} collective-permute-done((bf16[128,10,10,1]{0,3,2,1:T(2,128)(2,1)S(1)}, bf16[128,10,10,1]{0,3,2,1:T(2,128)(2,1)S(1)}, u32[]{:S(2)}, u32[]{:S(2)}) %collective-permute-start.11) | collective-permute-done | bytes 25632 | tf_op jit(solution)/shard_map/ppermute | solution.py:24
  251.3 3.0 maximum_convert_fusion.1
  254.3 4.5 %fusion.15 = bf16[128,8,8,128]{0,3,2,1:T(8,128)(2,1)S(1)} fusion(f32[128,8,8,128]{0,3,2,1:T(8,128)S(1)} %copy-done, f32[128,10,10,130]{0,3,2,1:T(8,128)S(1)} %maximum_convert_fusion.1, bf16[128,8,8,128]{0,3,2,1:T(8,128)(2,1)S(1)} %get-tuple-element.28, f32[8,8,128]{2,1,0:T(8,128)S(1)} %broadcast_add_fusion), kind=kLoop, calls=%fused_computation.38 | loop fusion | flops 13631488 | bytes 33587200 | tf_op jit(solution)/shard_map/convert_element_type | solution.py:35
  258.9 3.1 collective-permute-start.12
  265.3 3.8 %collective-permute-done.13 = bf16[128,1,8,128]{0,3,2,1:T(8,128)(2,1)S(1)} collective-permute-done((bf16[128,1,8,128]{0,3,2,1:T(8,128)(2,1)S(1)}, bf16[128,1,8,128]{0,3,2,1:T(8,128)(2,1)S(1)}, u32[]{:S(2)}, u32[]{:S(2)}) %collective-permute-start.13) | collective-permute-done | bytes 262176 | tf_op jit(solution)/shard_map/ppermute | solution.py:24
  269.2 4.6 %collective-permute-start.14 = (bf16[128,10,1,128]{0,3,2,1:T(8,128)(2,1)S(1)}, bf16[128,10,1,128]{0,3,2,1:T(8,128)(2,1)S(1)}, u32[]{:S(2)}, u32[]{:S(2)}) collective-permute-start(bf16[128,10,1,128]{0,3,2,1:T(8,128)(2,1)S(1)} %get-tuple-element.12), channel_id=1, source_target_pairs={{0,4},{4,8},{8,12},{12,16},{16,20},{20,24},{24,28},{28,32},{32,36}... | collective-permute-start | bytes 983048 | tf_op jit(solution)/shard_map/ppermute | solution.py:23
  273.8 3.4 %collective-permute-start.15 = (bf16[128,10,1,128]{0,3,2,1:T(8,128)(2,1)S(1)}, bf16[128,10,1,128]{0,3,2,1:T(8,128)(2,1)S(1)}, u32[]{:S(2)}, u32[]{:S(2)}) collective-permute-start(bf16[128,10,1,128]{0,3,2,1:T(8,128)(2,1)S(1)} %get-tuple-element.13), channel_id=1, source_target_pairs={{4,0},{8,4},{12,8},{16,12},{20,16},{24,20},{28,24},{32,28},{36,32}... | collective-permute-start | bytes 983048 | tf_op jit(solution)/shard_map/ppermute | solution.py:24
  277.2 5.4 %collective-permute-done.14 = bf16[128,10,1,128]{0,3,2,1:T(8,128)(2,1)S(1)} collective-permute-done((bf16[128,10,1,128]{0,3,2,1:T(8,128)(2,1)S(1)}, bf16[128,10,1,128]{0,3,2,1:T(8,128)(2,1)S(1)}, u32[]{:S(2)}, u32[]{:S(2)}) %collective-permute-start.14) | collective-permute-done | bytes 327712 | tf_op jit(solution)/shard_map/ppermute | solution.py:23
  282.6 4.6 %collective-permute-done.15 = bf16[128,10,1,128]{0,3,2,1:T(8,128)(2,1)S(1)} collective-permute-done((bf16[128,10,1,128]{0,3,2,1:T(8,128)(2,1)S(1)}, bf16[128,10,1,128]{0,3,2,1:T(8,128)(2,1)S(1)}, u32[]{:S(2)}, u32[]{:S(2)}) %collective-permute-start.15) | collective-permute-done | bytes 327712 | tf_op jit(solution)/shard_map/ppermute | solution.py:24
  291.6 6.9 %collective-permute-done.17 = bf16[128,10,10,1]{0,3,2,1:T(2,128)(2,1)S(1)} collective-permute-done((bf16[128,10,10,1]{0,3,2,1:T(2,128)(2,1)S(1)}, bf16[128,10,10,1]{0,3,2,1:T(2,128)(2,1)S(1)}, u32[]{:S(2)}, u32[]{:S(2)}) %collective-permute-start.17) | collective-permute-done | bytes 25632 | tf_op jit(solution)/shard_map/ppermute | solution.py:24
  298.5 3.0 maximum_convert_fusion.2
  301.4 4.5 %fusion.16 = bf16[128,8,8,128]{0,3,2,1:T(8,128)(2,1)S(1)} fusion(f32[128,8,8,128]{0,3,2,1:T(8,128)S(1)} %copy-done, f32[128,10,10,130]{0,3,2,1:T(8,128)S(1)} %maximum_convert_fusion.2, bf16[128,8,8,128]{0,3,2,1:T(8,128)(2,1)S(1)} %fusion.15, f32[8,8,128]{2,1,0:T(8,128)S(1)} %broadcast_add_fusion), kind=kLoop, calls=%fused_computation.39 | loop fusion | flops 13631488 | bytes 33587200 | tf_op jit(solution)/shard_map/convert_element_type | solution.py:35
  (50 shorter events, 30.3 us)
Async XLA Ops:
  7.2 89.1 %all-gather.2.cloned.1.call-start = ((), (), s32[]{:S(2)}) async-start(), calls=%async_computation.2 | async-start | bytes 4456448 | tf_op jit(solution)/shard_map/all_gather | solution.py:56
  15.5 12.7 %copy-start.1 = (f32[8,8,128]{2,1,0:T(8,128)S(1)}, f32[8,8,128]{2,1,0:T(8,128)}, u32[]{:S(2)}) copy-start(f32[8,8,128]{2,1,0:T(8,128)} %param.8) | copy-start | bytes 98308
  15.5 144.8 %reduce-scatter.2.cloned.1.call-start = ((), (), s32[]{:S(2)}) async-start(), calls=%async_computation.3 | async-start | bytes 139264 | tf_op jit(solution)/shard_map/reduce_scatter | solution.py:64
  19.0 9.2 %collective-permute-start = (bf16[128,1,8,128]{0,3,2,1:T(8,128)(2,1)S(1)}, bf16[128,1,8,128]{0,3,2,1:T(8,128)(2,1)S(1)}, u32[]{:S(2)}, u32[]{:S(2)}) collective-permute-start(bf16[128,1,8,128]{0,3,2,1:T(8,128)(2,1)S(1)} %get-tuple-element.22), channel_id=1, source_target_pairs={{0,64},{64,128},{128,192},{1,65},{65,129},{129,193},{2,66},{66,130... | collective-permute-start | bytes 786440 | tf_op jit(solution)/shard_map/ppermute | solution.py:23
  22.1 8.8 %collective-permute-start.1 = (bf16[128,1,8,128]{0,3,2,1:T(8,128)(2,1)S(1)}, bf16[128,1,8,128]{0,3,2,1:T(8,128)(2,1)S(1)}, u32[]{:S(2)}, u32[]{:S(2)}) collective-permute-start(bf16[128,1,8,128]{0,3,2,1:T(8,128)(2,1)S(1)} %get-tuple-element.23), channel_id=1, source_target_pairs={{64,0},{128,64},{192,128},{65,1},{129,65},{193,129},{66,2},{130,66... | collective-permute-start | bytes 786440 | tf_op jit(solution)/shard_map/ppermute | solution.py:24
  31.8 71.1 %collective-permute-start.2 = (bf16[128,10,1,128]{0,3,2,1:T(8,128)(2,1)}, bf16[128,10,1,128]{0,3,2,1:T(8,128)(2,1)S(1)}, u32[]{:S(2)}, u32[]{:S(2)}) collective-permute-start(bf16[128,10,1,128]{0,3,2,1:T(8,128)(2,1)} %get-tuple-element.16), channel_id=1, source_target_pairs={{0,4},{4,8},{8,12},{12,16},{16,20},{20,24},{24,28},{28,32},{32,36}... | collective-permute-start | bytes 983048 | tf_op jit(solution)/shard_map/ppermute | solution.py:23
  35.4 67.6 %collective-permute-start.3 = (bf16[128,10,1,128]{0,3,2,1:T(8,128)(2,1)}, bf16[128,10,1,128]{0,3,2,1:T(8,128)(2,1)S(1)}, u32[]{:S(2)}, u32[]{:S(2)}) collective-permute-start(bf16[128,10,1,128]{0,3,2,1:T(8,128)(2,1)} %get-tuple-element.17), channel_id=1, source_target_pairs={{4,0},{8,4},{12,8},{16,12},{20,16},{24,20},{28,24},{32,28},{36,32}... | collective-permute-start | bytes 983048 | tf_op jit(solution)/shard_map/ppermute | solution.py:24
  103.1 75.9 %collective-permute-start.4 = (bf16[128,10,10,1]{0,3,2,1:T(2,128)(2,1)S(1)}, bf16[128,10,10,1]{0,3,2,1:T(2,128)(2,1)S(1)}, u32[]{:S(2)}, u32[]{:S(2)}) collective-permute-start(bf16[128,10,10,1]{0,3,2,1:T(2,128)(2,1)S(1)} %get-tuple-element.10), channel_id=1, source_target_pairs={{0,1},{1,2},{2,3},{4,5},{5,6},{6,7},{8,9},{9,10},{10,11},{12,13},{... | collective-permute-start | bytes 76808 | tf_op jit(solution)/shard_map/ppermute | solution.py:23
  105.0 74.0 %collective-permute-start.5 = (bf16[128,10,10,1]{0,3,2,1:T(2,128)(2,1)S(1)}, bf16[128,10,10,1]{0,3,2,1:T(2,128)(2,1)S(1)}, u32[]{:S(2)}, u32[]{:S(2)}) collective-permute-start(bf16[128,10,10,1]{0,3,2,1:T(2,128)(2,1)S(1)} %get-tuple-element.11), channel_id=1, source_target_pairs={{1,0},{2,1},{3,2},{5,4},{6,5},{7,6},{9,8},{10,9},{11,10},{13,12},{... | collective-permute-start | bytes 76808 | tf_op jit(solution)/shard_map/ppermute | solution.py:24
  161.8 24.2 %all-to-all-start = ((f32[4,1,128]{2,1,0:T(1,128)}), f32[4,1,128]{2,1,0:T(1,128)}, u32[]{:S(2)}, u32[]{:S(2)}) async-start(f32[4,1,128]{2,1,0:T(1,128)} %reshape.42), calls=%async_computation.1 | async-start | bytes 4096 | tf_op jit(solution)/shard_map/all_to_all | solution.py:12
  179.0 9.2 %copy-start.2 = (s32[8,8,128]{2,1,0:T(8,128)S(1)}, s32[8,8,128]{2,1,0:T(8,128)}, u32[]{:S(2)}) copy-start(s32[8,8,128]{2,1,0:T(8,128)} %multiply_add_fusion) | copy-start | bytes 98308
  179.0 9.2 %copy-start.3 = (s32[1,1,1,4]{3,2,1,0:T(1,128)S(1)}, s32[1,1,1,4]{3,2,1,0:T(1,128)}, u32[]{:S(2)}) copy-start(s32[1,1,1,4]{3,2,1,0:T(1,128)} %param.11) | copy-start | bytes 52
  202.3 8.2 %collective-permute-start.6 = (bf16[128,1,8,128]{0,3,2,1:T(8,128)(2,1)S(1)}, bf16[128,1,8,128]{0,3,2,1:T(8,128)(2,1)S(1)}, u32[]{:S(2)}, u32[]{:S(2)}) collective-permute-start(bf16[128,1,8,128]{0,3,2,1:T(8,128)(2,1)S(1)} %get-tuple-element.20), channel_id=1, source_target_pairs={{0,64},{64,128},{128,192},{1,65},{65,129},{129,193},{2,66},{66,130... | collective-permute-start | bytes 786440 | tf_op jit(solution)/shard_map/ppermute | solution.py:23
  205.4 8.9 %collective-permute-start.7 = (bf16[128,1,8,128]{0,3,2,1:T(8,128)(2,1)S(1)}, bf16[128,1,8,128]{0,3,2,1:T(8,128)(2,1)S(1)}, u32[]{:S(2)}, u32[]{:S(2)}) collective-permute-start(bf16[128,1,8,128]{0,3,2,1:T(8,128)(2,1)S(1)} %get-tuple-element.21), channel_id=1, source_target_pairs={{64,0},{128,64},{192,128},{65,1},{129,65},{193,129},{66,2},{130,66... | collective-permute-start | bytes 786440 | tf_op jit(solution)/shard_map/ppermute | solution.py:24
  214.4 12.2 %collective-permute-start.8 = (bf16[128,10,1,128]{0,3,2,1:T(8,128)(2,1)S(1)}, bf16[128,10,1,128]{0,3,2,1:T(8,128)(2,1)S(1)}, u32[]{:S(2)}, u32[]{:S(2)}) collective-permute-start(bf16[128,10,1,128]{0,3,2,1:T(8,128)(2,1)S(1)} %get-tuple-element.14), channel_id=1, source_target_pairs={{0,4},{4,8},{8,12},{12,16},{16,20},{20,24},{24,28},{28,32},{32,36}... | collective-permute-start | bytes 983048 | tf_op jit(solution)/shard_map/ppermute | solution.py:23
  217.3 16.7 %collective-permute-start.9 = (bf16[128,10,1,128]{0,3,2,1:T(8,128)(2,1)S(1)}, bf16[128,10,1,128]{0,3,2,1:T(8,128)(2,1)S(1)}, u32[]{:S(2)}, u32[]{:S(2)}) collective-permute-start(bf16[128,10,1,128]{0,3,2,1:T(8,128)(2,1)S(1)} %get-tuple-element.15), channel_id=1, source_target_pairs={{4,0},{8,4},{12,8},{16,12},{20,16},{24,20},{28,24},{32,28},{36,32}... | collective-permute-start | bytes 983048 | tf_op jit(solution)/shard_map/ppermute | solution.py:24
  234.1 9.8 %collective-permute-start.10 = (bf16[128,10,10,1]{0,3,2,1:T(2,128)(2,1)S(1)}, bf16[128,10,10,1]{0,3,2,1:T(2,128)(2,1)S(1)}, u32[]{:S(2)}, u32[]{:S(2)}) collective-permute-start(bf16[128,10,10,1]{0,3,2,1:T(2,128)(2,1)S(1)} %get-tuple-element.8), channel_id=1, source_target_pairs={{0,1},{1,2},{2,3},{4,5},{5,6},{6,7},{8,9},{9,10},{10,11},{12,13},{... | collective-permute-start | bytes 76808 | tf_op jit(solution)/shard_map/ppermute | solution.py:23
  241.7 12.6 %copy-start = (f32[128,8,8,128]{0,3,2,1:T(8,128)S(1)}, f32[128,8,8,128]{0,3,2,1:T(8,128)}, u32[]{:S(2)}) copy-start(f32[128,8,8,128]{0,3,2,1:T(8,128)} %get-tuple-element.29) | copy-start | bytes 12582916
  241.7 9.6 %collective-permute-start.11 = (bf16[128,10,10,1]{0,3,2,1:T(2,128)(2,1)S(1)}, bf16[128,10,10,1]{0,3,2,1:T(2,128)(2,1)S(1)}, u32[]{:S(2)}, u32[]{:S(2)}) collective-permute-start(bf16[128,10,10,1]{0,3,2,1:T(2,128)(2,1)S(1)} %get-tuple-element.9), channel_id=1, source_target_pairs={{1,0},{2,1},{3,2},{5,4},{6,5},{7,6},{9,8},{10,9},{11,10},{13,12},{... | collective-permute-start | bytes 76808 | tf_op jit(solution)/shard_map/ppermute | solution.py:24
  258.9 6.4 %collective-permute-start.12 = (bf16[128,1,8,128]{0,3,2,1:T(8,128)(2,1)S(1)}, bf16[128,1,8,128]{0,3,2,1:T(8,128)(2,1)S(1)}, u32[]{:S(2)}, u32[]{:S(2)}) collective-permute-start(bf16[128,1,8,128]{0,3,2,1:T(8,128)(2,1)S(1)} %get-tuple-element.18), channel_id=1, source_target_pairs={{0,64},{64,128},{128,192},{1,65},{65,129},{129,193},{2,66},{66,130... | collective-permute-start | bytes 786440 | tf_op jit(solution)/shard_map/ppermute | solution.py:23
  262.0 7.1 %collective-permute-start.13 = (bf16[128,1,8,128]{0,3,2,1:T(8,128)(2,1)S(1)}, bf16[128,1,8,128]{0,3,2,1:T(8,128)(2,1)S(1)}, u32[]{:S(2)}, u32[]{:S(2)}) collective-permute-start(bf16[128,1,8,128]{0,3,2,1:T(8,128)(2,1)S(1)} %get-tuple-element.19), channel_id=1, source_target_pairs={{64,0},{128,64},{192,128},{65,1},{129,65},{193,129},{66,2},{130,66... | collective-permute-start | bytes 786440 | tf_op jit(solution)/shard_map/ppermute | solution.py:24
  269.2 13.4 %collective-permute-start.14 = (bf16[128,10,1,128]{0,3,2,1:T(8,128)(2,1)S(1)}, bf16[128,10,1,128]{0,3,2,1:T(8,128)(2,1)S(1)}, u32[]{:S(2)}, u32[]{:S(2)}) collective-permute-start(bf16[128,10,1,128]{0,3,2,1:T(8,128)(2,1)S(1)} %get-tuple-element.12), channel_id=1, source_target_pairs={{0,4},{4,8},{8,12},{12,16},{16,20},{20,24},{24,28},{28,32},{32,36}... | collective-permute-start | bytes 983048 | tf_op jit(solution)/shard_map/ppermute | solution.py:23
  273.8 13.4 %collective-permute-start.15 = (bf16[128,10,1,128]{0,3,2,1:T(8,128)(2,1)S(1)}, bf16[128,10,1,128]{0,3,2,1:T(8,128)(2,1)S(1)}, u32[]{:S(2)}, u32[]{:S(2)}) collective-permute-start(bf16[128,10,1,128]{0,3,2,1:T(8,128)(2,1)S(1)} %get-tuple-element.13), channel_id=1, source_target_pairs={{4,0},{8,4},{12,8},{16,12},{20,16},{24,20},{28,24},{32,28},{36,32}... | collective-permute-start | bytes 983048 | tf_op jit(solution)/shard_map/ppermute | solution.py:24
  287.2 4.3 %collective-permute-start.16 = (bf16[128,10,10,1]{0,3,2,1:T(2,128)(2,1)S(1)}, bf16[128,10,10,1]{0,3,2,1:T(2,128)(2,1)S(1)}, u32[]{:S(2)}, u32[]{:S(2)}) collective-permute-start(bf16[128,10,10,1]{0,3,2,1:T(2,128)(2,1)S(1)} %get-tuple-element.6), channel_id=1, source_target_pairs={{0,1},{1,2},{2,3},{4,5},{5,6},{6,7},{8,9},{9,10},{10,11},{12,13},{... | collective-permute-start | bytes 76808 | tf_op jit(solution)/shard_map/ppermute | solution.py:23
  289.1 9.3 %collective-permute-start.17 = (bf16[128,10,10,1]{0,3,2,1:T(2,128)(2,1)S(1)}, bf16[128,10,10,1]{0,3,2,1:T(2,128)(2,1)S(1)}, u32[]{:S(2)}, u32[]{:S(2)}) collective-permute-start(bf16[128,10,10,1]{0,3,2,1:T(2,128)(2,1)S(1)} %get-tuple-element.7), channel_id=1, source_target_pairs={{1,0},{2,1},{3,2},{5,4},{6,5},{7,6},{9,8},{10,9},{11,10},{13,12},{... | collective-permute-start | bytes 76808 | tf_op jit(solution)/shard_map/ppermute | solution.py:24
Sparse Core Ops, SparseCore 0:
  15.7 80.5 all-gather.1
  103.1 57.2 reduce-scatter.1
